TPU v7x, 256 devices: a whole 4x4x8 slice. The times are simulated.
256 devices in a mesh: dp: 8 (over z), vocab: 32 (over y, x, core).
Axes of the slice: x: 4, y: 4, z: 8, core: 2. Of those that a mesh axis runs over, the one named last changes fastest.
Arguments:
- hidden: bfloat16 [5120, 4096], P(('dp', 'vocab')), may hold values from -192 to 192, as said below
- out_weight: bfloat16 [4096, 81920], P('dp', 'vocab'), may hold values from -0.09375 to 0.09375
- labels: int32 [5120], P('dp'), may hold values from 0 to 81919
- text_mask: int32 [5120], P('dp'), may hold values from 0 to 1, as said below
Outputs:
- token_loss: float32 [5120], P('dp')
- mean_loss: float32 [], replicated
Inputs may be any that keep to these rules, and one draw needn't show every extreme that they name: The hidden states are of moderate size in most rows, possibly larger in a few. `text_mask`: vision and text tokens come in runs of 16 aligned tokens.
All inputs are finite; a program needn't handle non-finite values.
Results may differ from a plain program's by a relative error of at most 0.0003.
Values may be sent and summed in bfloat16 or wider, within the bound.
A program may use at most 128 MiB of HBM per device.

v0:
```python
import jax
import jax.numpy as jnp
from jax import lax
from jax.sharding import PartitionSpec as P


def from_everyone(x, axis):
    devices = lax.axis_size(axis)
    return lax.all_to_all(jnp.broadcast_to(x[None], (devices, *x.shape)), axis, 0, 0, tiled=True)


def collected_together(x, axis):
    leaves = jax.tree.leaves(x)
    order = sorted(range(len(leaves)), key=lambda k: -leaves[k].size)
    width = (1, *leaves[order[0]].shape)[-1]
    lines = [
        jnp.pad(leaves[k].reshape(-1), (0, -leaves[k].size % width)).reshape(-1, width)
        for k in order
    ]
    both, at, found = (from_everyone(jnp.concatenate(lines), axis), 0, {})
    for k, line in zip(order, lines):
        slab = both[:, at : at + len(line)].reshape(len(both), -1)
        found[k] = slab[:, : leaves[k].size].reshape(-1, *leaves[k].shape)
        at += len(line)
    numbers = iter(range(len(leaves)))
    return jax.tree.map(lambda _: found[next(numbers)], x)


def joined_by_halves(pieces, combine):
    while len(jax.tree.leaves(pieces)[0]) > 1:
        pieces = jax.vmap(combine)(
            *(jax.tree.map(lambda part: part[side::2], pieces) for side in (0, 1))
        )
    return jax.tree.map(lambda part: part[0], pieces)


def joined_all(x, axis, combine):
    pieces = collected_together(x, axis)
    return joined_by_halves(pieces, combine)


def over_copies(x, axis):
    return from_everyone(x, axis).sum(axis=0)


def packed_total(arrays, axis):
    line, at, done = (jnp.concatenate([a.reshape(-1) for a in arrays]), 0, [])
    so_far = over_copies(line, axis)
    for a in arrays:
        done.append(so_far[at : at + a.size].reshape(a.shape))
        at += a.size
    return tuple(done)


def shards(hidden, out_weight, labels, text_mask):
    gathered = lax.all_gather(hidden, "vocab", axis=0, tiled=True)
    width_here = out_weight.shape[1]
    first_column = lax.axis_index("vocab") * width_here
    weight_full = lax.all_gather(out_weight, "dp", axis=0, tiled=True)
    logits = jnp.dot(gathered, weight_full, preferred_element_type=jnp.float32)
    columns = jnp.arange(width_here, dtype=jnp.int32)
    local_targets = labels - first_column
    picked = jnp.sum(
        jnp.where(columns[None, :] == local_targets[:, None], logits, jnp.float32(0.0)), axis=1
    )
    local_top = jnp.max(logits, axis=1)
    weights_text = text_mask.astype(jnp.float32)
    local_total = jnp.sum(jnp.exp(logits - local_top[:, None]), axis=1)

    def combine(first, second):
        upper = jnp.maximum(first[0], second[0])
        summed = first[1] * jnp.exp(first[0] - upper) + second[1] * jnp.exp(second[0] - upper)
        return (upper, summed, first[2] + second[2])

    row_top, exp_total, label_logit = joined_all((local_top, local_total, picked), "vocab", combine)
    token_loss = weights_text * (row_top + jnp.log(exp_total) - label_logit)
    loss_sum, tally = packed_total((jnp.sum(token_loss), jnp.sum(weights_text)), "dp")
    mean_loss = loss_sum / jnp.maximum(tally, jnp.float32(1.0))
    return (token_loss, mean_loss)


def solution(mesh):
    in_specs = (P(("dp", "vocab"), None), P("dp", "vocab"), P("dp"), P("dp"))
    out_specs = (P("dp"), P())
    return jax.shard_map(shards, mesh=mesh, in_specs=in_specs, out_specs=out_specs, check_vma=False)
```

profile of v0, /device:TPU:1, one launch (start us, length us, event | category | flops | bytes accessed | tf_op | source)
XLA Modules:
  0.0 342.3 jit_solution(15762076118572349161)
XLA Ops:
  7.2 0.0 all-gather.6.cloned.1.call-start
  7.2 0.7 all-gather.6.cloned.1.call-update
  7.9 0.0 all-gather.4.cloned.1.call-start
  7.9 0.7 all-gather.4.cloned.1.call-update
  8.7 0.7 broadcast_subtract_fusion
  9.3 59.4 %all-gather.6.cloned.1.call-done = bf16[32,20,4096]{2,1,0:T(8,128)(2,1)} async-done(((bf16[1,20,4096]{2,1,0:T(8,128)(2,1)}), bf16[32,20,4096]{2,1,0:T(8,128)(2,1)}) %all-gather.6.cloned.1.call-update) | async-done | bytes 5242896 | tf_op jit(solution)/shard_map/all_gather | solution.py:56
  68.7 7.8 %reshape.54 = bf16[640,4096]{1,0:T(8,128)(2,1)} reshape(bf16[32,20,4096]{2,1,0:T(8,128)(2,1)} %all-gather.6.cloned.1.call-done) | data formatting | bytes 10485760
  76.5 204.4 %all-gather.4.cloned.1.call-done = bf16[4096,2560]{1,0:T(8,128)(2,1)} async-done(((bf16[512,2560]{1,0:T(8,128)(2,1)}), bf16[4096,2560]{1,0:T(8,128)(2,1)}) %all-gather.4.cloned.1.call-update) | async-done | bytes 20971536 | tf_op jit(solution)/shard_map/all_gather | solution.py:59
  280.9 18.6 %fusion.7 = (f32[640]{0:T(1024)S(1)}, f32[640,2560]{1,0:T(8,128)S(1)}) fusion(bf16[640,4096]{1,0:T(8,128)(2,1)} %reshape.54, bf16[4096,2560]{1,0:T(8,128)(2,1)} %all-gather.4.cloned.1.call-done), kind=kOutput, calls=%fused_computation.26 | convolution fusion | flops 13423410176 | bytes 32770560 | tf_op jit(solution)/shard_map/dot_general | solution.py:60
  299.5 0.0 copy-start
  299.5 1.7 exponential_reduce_fusion
  301.3 17.0 %all_to_all.11 = f32[32,3,640]{2,1,0:T(4,128)S(1)} all-to-all(f32[32,3,640]{2,1,0:T(4,128)S(1)} %broadcast_in_dim.9), channel_id=1, replica_groups=mesh['dp'=8,'vocab'=32] {'vocab'}, dimensions={0} | all-to-all | bytes 491520 | tf_op jit(solution)/shard_map/all_to_all | solution.py:9
  318.3 0.2 fusion.5
  319.3 0.0 copy-done
  319.3 1.3 fusion.4
  320.6 1.4 pad_maximum_fusion.1
  322.0 10.4 %all_to_all.12 = f32[8,1,2]{2,1,0:T(1,128)S(1)} all-to-all(f32[8,1,2]{2,1,0:T(1,128)S(1)} %broadcast_in_dim.10), channel_id=1, replica_groups=mesh['dp'=8,'vocab'=32] {'dp'}, dimensions={0} | all-to-all | bytes 128 | tf_op jit(solution)/shard_map/all_to_all | solution.py:9
  332.4 0.6 fusion.6
  (42 shorter events, 0.8 us)
Async XLA Ops:
  7.2 61.5 %all-gather.6.cloned.1.call-start = ((), (), s32[]{:S(2)}) async-start(), calls=%async_computation.3 | async-start | bytes 6488064 | tf_op jit(solution)/shard_map/all_gather | solution.py:56
  7.9 273.0 %all-gather.4.cloned.1.call-start = ((), (), s32[]{:S(2)}) async-start(), calls=%async_computation.2 | async-start | bytes 23592960 | tf_op jit(solution)/shard_map/all_gather | solution.py:59
  299.5 19.8 %copy-start = (s32[640]{0:T(1024)S(1)}, s32[640]{0:T(1024)}, u32[]{:S(2)}) copy-start(s32[640]{0:T(1024)} %param.7) | copy-start | bytes 7684
Sparse Core Ops, SparseCore 0:
  10.5 58.1 all-gather.5
  70.5 210.3 all-gather.3
where the time goes:
time: 343 us; the launch traced here: 342 us
  waiting for transfers between devices  265 us (77%)
  blocking collectives  27.4 us (8%)
  matrix products  18.6 us (5%)
  between operations  16.7 us (5%)
  local copies, waits for them, and re-layouts  9.13 us (3%)
  other arithmetic  5.29 us (2%)
    all_gather x1, waiting for transfers between devices, shards(): weight_full = lax.all_gather(out_weight, 'dp', axis=0, tiled=True)  204 us
    all_gather x1, waiting for transfers between devices, shards(): gathered = lax.all_gather(hidden, 'vocab', axis=0, tiled=True)  59.4 us
    all_to_all x2, blocking collectives, from_everyone(): lax.all_to_all(jnp.broadcast_to(x[None], (devices, *x.shape)), axis, 0, 0...  27.4 us
    dot_general x1, matrix products, shards(): logits = jnp.dot(gathered, weight_full, preferred_element_type=jnp.float32)  18.6 us
    unnamed x4, local copies, waits for them, and re-layouts  7.78 us
  transfers between devices with their start and end apart: 2, of which 2 were waited for; matrix products, arithmetic and copies ran while one was open for 2% of the time, Pallas kernels for 0%

commit v1 on v0

--- a/solution.py
+++ b/solution.py
@@ -56,7 +56,23 @@
     gathered = lax.all_gather(hidden, "vocab", axis=0, tiled=True)
     width_here = out_weight.shape[1]
     first_column = lax.axis_index("vocab") * width_here
-    weight_full = lax.all_gather(out_weight, "dp", axis=0, tiled=True)
+    carry_in = lax.axis_size("dp")
+    main, next_value, new = (carry_in, lax.axis_index("dp"), out_weight.shape[0])
+    kept_rows = [i * main if jj == 0 else i for jj, i in enumerate(out_weight.shape)]
+    weight_full = lax.dynamic_update_slice_in_dim(
+        jnp.zeros(kept_rows, out_weight.dtype), out_weight, next_value * new, axis=0
+    )
+    current_arr = shaped = out_weight
+    for j in range(1, main // 2 + 1):
+        current_arr = lax.ppermute(current_arr, "dp", [(jj, (jj + 1) % main) for jj in range(main)])
+        weight_full = lax.dynamic_update_slice_in_dim(
+            weight_full, current_arr, (next_value - j) % main * new, axis=0
+        )
+        if 2 * j < main:
+            shaped = lax.ppermute(shaped, "dp", perm=[(jj, (jj - 1) % main) for jj in range(main)])
+            weight_full = lax.dynamic_update_slice_in_dim(
+                weight_full, shaped, (next_value + j) % main * new, axis=0
+            )
     logits = jnp.dot(gathered, weight_full, preferred_element_type=jnp.float32)
     columns = jnp.arange(width_here, dtype=jnp.int32)
     local_targets = labels - first_column

time: 343 us -> 315 us (0.918)
  waiting for transfers between devices: 265 us -> 189 us
  local copies, waits for them, and re-layouts: 9.13 us -> 38.6 us
  starting transfers between devices: 0.08 us -> 13.5 us
  blocking collectives: 27.4 us -> 31 us
    all_gather x1 -> x0, waiting for transfers between devices: 204 us -> none  [shards(): weight_full = lax.all_gather(out_weight, 'dp', axis=0, tiled=True)]
    ppermute x0 -> x7, waiting for transfers between devices: none -> 189 us  [the longest x4 189 us: shards(): lax.ppermute(current_arr, 'dp', [(jj, (jj + 1) % main) for jj in range(ma...]
    all_gather x1, waiting for transfers between devices: 59.4 us -> 0.01 us  [shards(): gathered = lax.all_gather(hidden, 'vocab', axis=0, tiled=True)]
    dynamic_update_slice x0 -> x8, local copies, waits for them, and re-layouts: none -> 22.1 us  [the longest x4 11.8 us: shards(): lax.dynamic_update_slice_in_dim(weight_full, current_arr, (next_value - j...]
    ppermute x0 -> x7, starting transfers between devices: none -> 13.4 us  [the longest x3 10.9 us: shards(): lax.ppermute(shaped, 'dp', perm=[(jj, (jj - 1) % main) for jj in range(ma...]
    broadcast_in_dim x0 -> x1, local copies, waits for them, and re-layouts: none -> 7.31 us  [shards(): jnp.zeros(kept_rows, out_weight.dtype)]
    all_to_all x2, blocking collectives: 27.4 us -> 31 us  [from_everyone(): lax.all_to_all(jnp.broadcast_to(x[None], (devices, *x.shape)), axis, 0, 0...]
    unnamed x4 -> x8, local copies, waits for them, and re-layouts: 7.78 us -> 7.84 us
  transfers between devices with their start and end apart: 2 -> 8, of which waited for: 2 -> 4; matrix products, arithmetic and copies ran while one was open for 2% -> 11% of each run, Pallas kernels for 0% -> 0%
where the time goes in v1:
time: 315 us
  waiting for transfers between devices  189 us (60%)
  local copies, waits for them, and re-layouts  38.6 us (12%)
  blocking collectives  31 us (10%)
  matrix products  21.2 us (7%)
  between operations  16.6 us (5%)
  starting transfers between devices  13.5 us (4%)
  other arithmetic  4.6 us (1%)
    ppermute x4, waiting for transfers between devices, shards(): lax.ppermute(current_arr, 'dp', [(jj, (jj + 1) % main) for jj in range(ma...  189 us
    all_to_all x2, blocking collectives, from_everyone(): lax.all_to_all(jnp.broadcast_to(x[None], (devices, *x.shape)), axis, 0, 0...  31 us
    dot_general x1, matrix products, shards(): logits = jnp.dot(gathered, weight_full, preferred_element_type=jnp.float32)  21.2 us
    dynamic_update_slice x4, local copies, waits for them, and re-layouts, shards(): lax.dynamic_update_slice_in_dim(weight_full, current_arr, (next_value - j...  11.8 us
    ppermute x3, starting transfers between devices, shards(): lax.ppermute(shaped, 'dp', perm=[(jj, (jj - 1) % main) for jj in range(ma...  10.9 us
    dynamic_update_slice x3, local copies, waits for them, and re-layouts, shards(): lax.dynamic_update_slice_in_dim(weight_full, shaped, (next_value + j) % m...  8.56 us
    unnamed x8, local copies, waits for them, and re-layouts  7.84 us
    broadcast_in_dim x1, local copies, waits for them, and re-layouts, shards(): jnp.zeros(kept_rows, out_weight.dtype)  7.31 us
  transfers between devices with their start and end apart: 8, of which 4 were waited for; matrix products, arithmetic and copies ran while one was open for 11% of the time, Pallas kernels for 0%

profile of v1, /device:TPU:1, one launch (start us, length us, event | category | flops | bytes accessed | tf_op | source)
XLA Modules:
  0.0 314.8 jit_solution(821959312679322440)
XLA Ops:
  7.2 0.0 all-gather.3.cloned.1.call-start
  7.2 2.5 collective-permute-start
  9.7 0.0 all-gather.3.cloned.1.call-update
  9.8 4.6 %collective-permute-start.1 = (bf16[512,2560]{1,0:T(8,128)(2,1)}, bf16[512,2560]{1,0:T(8,128)(2,1)}, u32[]{:S(2)}, u32[]{:S(2)}) collective-permute-start(bf16[512,2560]{1,0:T(8,128)(2,1)} %param.5), channel_id=1, source_target_pairs={{0,224},{32,0},{64,32},{96,64},{128,96},{160,128},{192,160},{224,1... | collective-permute-start | bytes 7864328 | tf_op jit(solution)/shard_map/ppermute | solution.py:72
  14.4 56.1 %collective-permute-done = bf16[512,2560]{1,0:T(8,128)(2,1)S(1)} collective-permute-done((bf16[512,2560]{1,0:T(8,128)(2,1)}, bf16[512,2560]{1,0:T(8,128)(2,1)S(1)}, u32[]{:S(2)}, u32[]{:S(2)}) %collective-permute-start) | collective-permute-done | bytes 2621472 | tf_op jit(solution)/shard_map/ppermute | solution.py:67
  70.5 0.0 collective-permute-start.2
  70.5 0.0 collective-permute-done.1
  70.5 3.2 %collective-permute-start.3 = (bf16[512,2560]{1,0:T(8,128)(2,1)}, bf16[512,2560]{1,0:T(8,128)(2,1)}, u32[]{:S(2)}, u32[]{:S(2)}) collective-permute-start(bf16[512,2560]{1,0:T(8,128)(2,1)} %collective-permute-done.1), channel_id=1, source_target_pairs={{0,224},{32,0},{64,32},{96,64},{128,96},{160,128},{192,160},{224,1... | collective-permute-start | bytes 7864328 | tf_op jit(solution)/shard_map/ppermute | solution.py:72
  73.6 55.3 %collective-permute-done.2 = bf16[512,2560]{1,0:T(8,128)(2,1)} collective-permute-done((bf16[512,2560]{1,0:T(8,128)(2,1)S(1)}, bf16[512,2560]{1,0:T(8,128)(2,1)}, u32[]{:S(2)}, u32[]{:S(2)}) %collective-permute-start.2) | collective-permute-done | bytes 2621472 | tf_op jit(solution)/shard_map/ppermute | solution.py:67
  128.9 0.0 collective-permute-start.4
  129.0 0.0 copy-start
  129.0 0.0 copy-start.1
  129.0 0.0 collective-permute-done.3
  129.0 3.1 collective-permute-start.5
  132.1 7.3 %broadcast_in_dim.10 = bf16[4096,2560]{1,0:T(8,128)(2,1)} broadcast(bf16[]{:T(256)} %constant.57.clone.1), dimensions={} | broadcast | bytes 20971522 | tf_op jit(solution)/shard_map/broadcast_in_dim | solution.py:63
  139.4 0.0 copy-done
  139.4 1.7 constant_dynamic-update-slice_fusion.7
  141.1 45.7 %collective-permute-done.4 = bf16[512,2560]{1,0:T(8,128)(2,1)} collective-permute-done((bf16[512,2560]{1,0:T(8,128)(2,1)}, bf16[512,2560]{1,0:T(8,128)(2,1)}, u32[]{:S(2)}, u32[]{:S(2)}) %collective-permute-start.4) | collective-permute-done | bytes 2621472 | tf_op jit(solution)/shard_map/ppermute | solution.py:67
  186.8 0.0 collective-permute-start.6
  186.8 0.0 copy-done.1
  186.8 1.6 constant_dynamic-update-slice_fusion.6
  188.4 3.4 %constant_dynamic-update-slice_fusion.5 = bf16[4096,2560]{1,0:T(8,128)(2,1)} fusion(bf16[4096,2560]{1,0:T(8,128)(2,1)} %constant_dynamic-update-slice_fusion.6, bf16[512,2560]{1,0:T(8,128)(2,1)} %collective-permute-done.1, s32[]{:T(128)S(6)} %select_n.63), kind=kLoop, calls=%fused_computation.30 | loop fusion | bytes 5242884 | tf_op jit(solution)/shard_map/dynamic_update_slice | solution.py:73
  191.9 3.4 %constant_dynamic-update-slice_fusion.4 = bf16[4096,2560]{1,0:T(8,128)(2,1)} fusion(bf16[4096,2560]{1,0:T(8,128)(2,1)} %constant_dynamic-update-slice_fusion.5, bf16[512,2560]{1,0:T(8,128)(2,1)} %collective-permute-done.2, s32[]{:T(128)S(6)} %select_n.65), kind=kLoop, calls=%fused_computation.29 | loop fusion | bytes 5242884 | tf_op jit(solution)/shard_map/dynamic_update_slice | solution.py:68
  195.3 3.4 %constant_dynamic-update-slice_fusion.3 = bf16[4096,2560]{1,0:T(8,128)(2,1)} fusion(bf16[4096,2560]{1,0:T(8,128)(2,1)} %constant_dynamic-update-slice_fusion.4, bf16[512,2560]{1,0:T(8,128)(2,1)} %collective-permute-done.3, s32[]{:T(128)S(6)} %select_n.67), kind=kLoop, calls=%fused_computation.28 | loop fusion | bytes 5242884 | tf_op jit(solution)/shard_map/dynamic_update_slice | solution.py:73
  198.7 3.4 %constant_dynamic-update-slice_fusion.2 = bf16[4096,2560]{1,0:T(8,128)(2,1)} fusion(bf16[4096,2560]{1,0:T(8,128)(2,1)} %constant_dynamic-update-slice_fusion.3, bf16[512,2560]{1,0:T(8,128)(2,1)} %collective-permute-done.4, s32[]{:T(128)S(6)} %select_n.69), kind=kLoop, calls=%fused_computation.27 | loop fusion | bytes 5242884 | tf_op jit(solution)/shard_map/dynamic_update_slice | solution.py:68
  202.1 0.0 collective-permute-done.5
  202.1 1.7 constant_dynamic-update-slice_fusion.1
  203.8 0.0 all-gather.3.cloned.1.call-done
  203.8 7.8 %reshape.54 = bf16[640,4096]{1,0:T(8,128)(2,1)} reshape(bf16[32,20,4096]{2,1,0:T(8,128)(2,1)} %all-gather.3.cloned.1.call-done) | data formatting | bytes 10485760
  211.6 32.2 %collective-permute-done.6 = bf16[512,2560]{1,0:T(8,128)(2,1)} collective-permute-done((bf16[512,2560]{1,0:T(8,128)(2,1)}, bf16[512,2560]{1,0:T(8,128)(2,1)}, u32[]{:S(2)}, u32[]{:S(2)}) %collective-permute-start.6) | collective-permute-done | bytes 2621472 | tf_op jit(solution)/shard_map/ppermute | solution.py:67
  243.8 3.4 %constant_dynamic-update-slice_fusion = bf16[4096,2560]{1,0:T(8,128)(2,1)} fusion(bf16[4096,2560]{1,0:T(8,128)(2,1)} %constant_dynamic-update-slice_fusion.1, bf16[512,2560]{1,0:T(8,128)(2,1)} %collective-permute-done.6, s32[]{:T(128)S(6)} %select_n.73), kind=kLoop, calls=%fused_computation.25 | loop fusion | bytes 5242884 | tf_op jit(solution)/shard_map/dynamic_update_slice | solution.py:68
  247.2 21.2 %fusion.10 = (f32[640]{0:T(1024)S(1)}, f32[2560,640]{1,0:T(8,128)S(1)}) fusion(bf16[4096,2560]{1,0:T(8,128)(2,1)} %constant_dynamic-update-slice_fusion, bf16[640,4096]{1,0:T(8,128)(2,1)} %reshape.54), kind=kOutput, calls=%fused_computation.37 | convolution fusion | flops 13423410176 | bytes 32770560 | tf_op jit(solution)/shard_map/dot_general | solution.py:76
  268.4 0.0 copy-start.2
  268.4 1.8 fusion.1
  270.3 20.2 %all_to_all.11 = f32[32,3,640]{2,1,0:T(4,128)S(1)} all-to-all(f32[32,3,640]{2,1,0:T(4,128)S(1)} %broadcast_in_dim.12), channel_id=1, replica_groups=mesh['dp'=8,'vocab'=32] {'vocab'}, dimensions={0} | all-to-all | bytes 491520 | tf_op jit(solution)/shard_map/all_to_all | solution.py:9
  290.5 0.2 fusion.8
  291.5 0.0 copy-done.2
  291.5 1.3 fusion.7
  292.8 1.4 pad_maximum_fusion.1
  294.1 10.8 %all_to_all.12 = f32[8,1,2]{2,1,0:T(1,128)S(1)} all-to-all(f32[8,1,2]{2,1,0:T(1,128)S(1)} %broadcast_in_dim.13), channel_id=1, replica_groups=mesh['dp'=8,'vocab'=32] {'dp'}, dimensions={0} | all-to-all | bytes 128 | tf_op jit(solution)/shard_map/all_to_all | solution.py:9
  304.9 0.6 fusion.9
  (43 shorter events, 0.8 us)
Async XLA Ops:
  7.2 196.6 %all-gather.3.cloned.1.call-start = ((), (), s32[]{:S(2)}) async-start(), calls=%async_computation.2 | async-start | bytes 6488064 | tf_op jit(solution)/shard_map/all_gather | solution.py:56
  7.2 63.2 %collective-permute-start = (bf16[512,2560]{1,0:T(8,128)(2,1)}, bf16[512,2560]{1,0:T(8,128)(2,1)S(1)}, u32[]{:S(2)}, u32[]{:S(2)}) collective-permute-start(bf16[512,2560]{1,0:T(8,128)(2,1)} %param.5), channel_id=1, source_target_pairs={{0,32},{32,64},{64,96},{96,128},{128,160},{160,192},{192,224},{224... | collective-permute-start | bytes 7864328 | tf_op jit(solution)/shard_map/ppermute | solution.py:67
  9.8 60.7 %collective-permute-start.1 = (bf16[512,2560]{1,0:T(8,128)(2,1)}, bf16[512,2560]{1,0:T(8,128)(2,1)}, u32[]{:S(2)}, u32[]{:S(2)}) collective-permute-start(bf16[512,2560]{1,0:T(8,128)(2,1)} %param.5), channel_id=1, source_target_pairs={{0,224},{32,0},{64,32},{96,64},{128,96},{160,128},{192,160},{224,1... | collective-permute-start | bytes 7864328 | tf_op jit(solution)/shard_map/ppermute | solution.py:72
  70.5 58.5 %collective-permute-start.2 = (bf16[512,2560]{1,0:T(8,128)(2,1)S(1)}, bf16[512,2560]{1,0:T(8,128)(2,1)}, u32[]{:S(2)}, u32[]{:S(2)}) collective-permute-start(bf16[512,2560]{1,0:T(8,128)(2,1)S(1)} %collective-permute-done), channel_id=1, source_target_pairs={{0,32},{32,64},{64,96},{96,128},{128,160},{160,192},{192,224},{224... | collective-permute-start | bytes 7864328 | tf_op jit(solution)/shard_map/ppermute | solution.py:67
  70.5 58.5 %collective-permute-start.3 = (bf16[512,2560]{1,0:T(8,128)(2,1)}, bf16[512,2560]{1,0:T(8,128)(2,1)}, u32[]{:S(2)}, u32[]{:S(2)}) collective-permute-start(bf16[512,2560]{1,0:T(8,128)(2,1)} %collective-permute-done.1), channel_id=1, source_target_pairs={{0,224},{32,0},{64,32},{96,64},{128,96},{160,128},{192,160},{224,1... | collective-permute-start | bytes 7864328 | tf_op jit(solution)/shard_map/ppermute | solution.py:72
  128.9 57.8 %collective-permute-start.4 = (bf16[512,2560]{1,0:T(8,128)(2,1)}, bf16[512,2560]{1,0:T(8,128)(2,1)}, u32[]{:S(2)}, u32[]{:S(2)}) collective-permute-start(bf16[512,2560]{1,0:T(8,128)(2,1)} %collective-permute-done.2), channel_id=1, source_target_pairs={{0,32},{32,64},{64,96},{96,128},{128,160},{160,192},{192,224},{224... | collective-permute-start | bytes 7864328 | tf_op jit(solution)/shard_map/ppermute | solution.py:67
  129.0 10.4 %copy-start = (bf16[512,2560]{1,0:T(8,128)(2,1)S(1)}, bf16[512,2560]{1,0:T(8,128)(2,1)}, u32[]{:S(2)}) copy-start(bf16[512,2560]{1,0:T(8,128)(2,1)} %param.5) | copy-start | bytes 7864324
  129.0 57.8 %copy-start.1 = (s32[640]{0:T(1024)S(1)}, s32[640]{0:T(1024)}, u32[]{:S(2)}) copy-start(s32[640]{0:T(1024)} %param.6) | copy-start | bytes 7684
  129.0 73.1 %collective-permute-start.5 = (bf16[512,2560]{1,0:T(8,128)(2,1)}, bf16[512,2560]{1,0:T(8,128)(2,1)S(1)}, u32[]{:S(2)}, u32[]{:S(2)}) collective-permute-start(bf16[512,2560]{1,0:T(8,128)(2,1)} %collective-permute-done.3), channel_id=1, source_target_pairs={{0,224},{32,0},{64,32},{96,64},{128,96},{160,128},{192,160},{224,1... | collective-permute-start | bytes 7864328 | tf_op jit(solution)/shard_map/ppermute | solution.py:72
  186.8 57.0 %collective-permute-start.6 = (bf16[512,2560]{1,0:T(8,128)(2,1)}, bf16[512,2560]{1,0:T(8,128)(2,1)}, u32[]{:S(2)}, u32[]{:S(2)}) collective-permute-start(bf16[512,2560]{1,0:T(8,128)(2,1)} %collective-permute-done.4), channel_id=1, source_target_pairs={{0,32},{32,64},{64,96},{96,128},{128,160},{160,192},{192,224},{224... | collective-permute-start | bytes 7864328 | tf_op jit(solution)/shard_map/ppermute | solution.py:67
  268.4 23.1 %copy-start.2 = (s32[640]{0:T(1024)S(1)}, s32[640]{0:T(1024)}, u32[]{:S(2)}) copy-start(s32[640]{0:T(1024)} %param.7) | copy-start | bytes 7684
Sparse Core Ops, SparseCore 0:
  10.5 58.1 all-gather.2
